TPU v7x, 32 devices: a whole 2x2x4 slice. The times are simulated.
32 devices in a mesh: wide: 8 (over y, x, core), narrow: 4 (over z).
Axes of the slice: x: 2, y: 2, z: 4, core: 2. Of those that a mesh axis runs over, the one named last changes fastest.
Arguments:
- tokens: bfloat16 [16, 1024, 768], P('wide', 'narrow'), may hold values from -6 to 6
- step_ids: int32 [16], P('wide'), may hold values from 0 to 999
- prefix: int32 [16], P('wide'), may hold values from 1 to 1024, as said below
- keep_bits: int32 [16, 1024], P('wide'), may hold values 0 or 1
- ada_weight: bfloat16 [4608, 128], replicated, may hold values from -0.5 to 0.5
- ada_bias: float32 [4608], replicated, may hold values from -3 to 3
- norm1_gain: float32 [768], replicated, may hold values from 0.5 to 1.5
- qkv_weight: bfloat16 [768, 2304], replicated, may hold values from -0.21875 to 0.21875
- out_weight: bfloat16 [768, 768], replicated, may hold values from -6 to 6
- norm2_gain: float32 [768], replicated, may hold values from 0.5 to 1.5
- up_weight: bfloat16 [768, 3072], replicated, may hold values from -0.21875 to 0.21875
- up_bias: float32 [3072], replicated, may hold values from -3 to 3
- down_weight: bfloat16 [3072, 768], replicated, may hold values from -0.21875 to 0.21875
- down_bias: float32 [768], replicated, may hold values from -3 to 3
- cotangent: bfloat16 [16, 1024, 768], P('wide', 'narrow'), may hold values from -6 to 6
Outputs:
- out_tokens: bfloat16 [16, 1024, 768], P('wide', 'narrow')
- input_grad: bfloat16 [16, 1024, 768], P('wide', 'narrow')
- ada_weight_grad: float32 [4608, 128], replicated
- ada_bias_grad: float32 [4608], replicated
- norm1_gain_grad: float32 [768], replicated
- qkv_weight_grad: float32 [768, 2304], replicated
- out_weight_grad: float32 [768, 768], replicated
- norm2_gain_grad: float32 [768], replicated
- up_weight_grad: float32 [768, 3072], replicated
- up_bias_grad: float32 [3072], replicated
- down_weight_grad: float32 [3072, 768], replicated
- down_bias_grad: float32 [768], replicated
Inputs may be any that keep to these rules, and one draw needn't show every extreme that they name: Every prefix keeps at least the first position visible; of the 2 consecutive sequences of each index of wide, one has the whole length 1024 as prefix.
All inputs are finite; a program needn't handle non-finite values. No bound on the sum of `keep_bits` on one device may be relied on, other than what follows from the above.
Results may differ from a plain program's by a relative error of at most 0.015.
Values may be sent and summed in bfloat16 or wider, within the bound.
A program may use at most 192 MiB of HBM per device.

v0:
```python
import functools
import math
import jax
import jax.numpy as jnp
from jax import lax
from jax.sharding import PartitionSpec as P

HEAD = 64
TEMB = 128
MICRO = 2
norm_epsilon = 1e-05
gelu_coeff = 0.7978845608028654
masked_score = -1e30


def shifted(block, axis, distance):
    devices = range(lax.axis_size(axis))
    route = [((i - distance) % len(devices), i) for i in devices]
    return lax.ppermute(block, axis, route)


def time_embed(step_ids):
    halfway = TEMB // 2
    frequency = jnp.exp(jnp.arange(halfway, dtype=jnp.float32) * (-math.log(10000.0) / halfway))
    angles = step_ids.astype(jnp.float32)[:, None] * frequency[None, :]
    return jnp.concatenate([jnp.cos(angles), jnp.sin(angles)], axis=-1)


def rope_tables(positions):
    halfway = HEAD // 2
    inverse = jnp.exp(jnp.arange(halfway, dtype=jnp.float32) * (-2.0 * math.log(10000.0) / HEAD))
    angles = positions[:, None] * inverse[None, :]
    return (jnp.cos(angles), jnp.sin(angles))


def rotate(values, cosine_rows, sine_rows):
    halfway = values.shape[-1] // 2
    former = values[..., :halfway]
    latter = values[..., halfway:]
    cos_wide = cosine_rows[:, None, :]
    sin_wide = sine_rows[:, None, :]
    return jnp.concatenate(
        [former * cos_wide - latter * sin_wide, latter * cos_wide + former * sin_wide], axis=-1
    )


def rotate_back(incoming, cosine_rows, sine_rows):
    halfway = incoming.shape[-1] // 2
    former = incoming[..., :halfway]
    latter = incoming[..., halfway:]
    cos_wide = cosine_rows[:, None, :]
    sin_wide = sine_rows[:, None, :]
    return jnp.concatenate(
        [former * cos_wide + latter * sin_wide, latter * cos_wide - former * sin_wide], axis=-1
    )


def layer_norm(values, scaling):
    center = values - jnp.mean(values, axis=-1, keepdims=True)
    spread = jnp.mean(center * center, axis=-1, keepdims=True)
    return center * lax.rsqrt(spread + norm_epsilon) * scaling


def modulate(values, scaling, shift_rows, scale_rows):
    return layer_norm(values, scaling) * (1.0 + scale_rows) + shift_rows


def gelu_tanh(values):
    inner_arg = gelu_coeff * (values + 0.044715 * values * values * values)
    return 0.5 * values * (1.0 + jnp.tanh(inner_arg))


def pass_pairs(pair_block):
    return shifted(pair_block, "narrow", 1)


def pass_pairs_again(pair_block):
    return shifted(pair_block, "narrow", 1)


def pass_grads(grad_block):
    return shifted(grad_block.astype(jnp.bfloat16), "narrow", 1).astype(grad_block.dtype)


def add_trees(former_tree, latter_tree):
    return jax.tree.map(jnp.add, former_tree, latter_tree)


def local(
    tokens,
    step_ids,
    prefix,
    keep_bits,
    ada_weight,
    ada_bias,
    norm1_gain,
    qkv_weight,
    out_weight,
    norm2_gain,
    up_weight,
    up_bias,
    down_weight,
    down_bias,
    cotangent,
):
    cycle_size = lax.axis_size("narrow")
    cycle_index = lax.axis_index("narrow")
    groups, span_size, width = tokens.shape
    per_micro = groups // MICRO
    head_count = width // HEAD
    score_scale = HEAD ** (-0.5)
    offsets = jnp.arange(span_size, dtype=jnp.int32)
    cosine_rows, sine_rows = rope_tables((cycle_index * span_size + offsets).astype(jnp.float32))
    condition = jax.nn.silu(time_embed(step_ids))
    modulation = (
        jnp.dot(
            condition,
            ada_weight.astype(jnp.float32).T,
            precision=lax.Precision.HIGHEST,
            preferred_element_type=jnp.float32,
        )
        + ada_bias
    )
    last_source = (cycle_index + 1) % cycle_size
    outputs = []
    input_grads = []
    collected = []
    for micro_index in range(MICRO):
        picked = slice(micro_index * per_micro, (micro_index + 1) * per_micro)
        inputs = tokens[picked].astype(jnp.float32)
        leading = prefix[picked]
        bits_here = keep_bits[picked]
        shift_one, scale_one, gate_one, shift_two, scale_two, gate_two = jnp.split(
            modulation[picked][:, None, :], 6, axis=-1
        )
        normed, norm_back = jax.vjp(modulate, inputs, norm1_gain, shift_one, scale_one)
        normed_low = normed.astype(jnp.bfloat16)
        projected = jnp.einsum(
            "bcd,de->bce", normed_low, qkv_weight, preferred_element_type=jnp.float32
        )
        shaped = projected.reshape(per_micro, span_size, 3, head_count, HEAD)
        queries = rotate(shaped[:, :, 0], cosine_rows, sine_rows).astype(jnp.bfloat16)
        key_rows = (
            rotate(shaped[:, :, 1], cosine_rows, sine_rows)
            .astype(jnp.bfloat16)
            .reshape(per_micro, span_size, width)
        )
        value_rows = shaped[:, :, 2].astype(jnp.bfloat16).reshape(per_micro, span_size, width)
        pair_rows = jnp.stack([key_rows, value_rows])

        def visible_keys(source):
            first_key = source * span_size
            window = lax.dynamic_slice_in_dim(bits_here, first_key, span_size, 1)
            allowed = ((first_key + offsets)[None, :] < leading[:, None]) | (window == 1)
            return allowed[:, None, None, :]

        def key_scores(key_block):
            shaped_keys = key_block.reshape(per_micro, span_size, head_count, HEAD)
            return (
                jnp.einsum(
                    "bqhe,bkhe->bhqk", queries, shaped_keys, preferred_element_type=jnp.float32
                )
                * score_scale
            )

        def add_online(pair_block, source, running):
            highest, total_sum, summed = running
            scores = key_scores(pair_block[0])
            allowed = visible_keys(source)
            block_high = jnp.max(jnp.where(allowed, scores, masked_score), axis=-1)
            new_high = jnp.maximum(highest, block_high)
            factor = jnp.exp(highest - new_high)
            exp_terms = jnp.where(allowed, jnp.exp(scores - new_high[..., None]), 0.0)
            total_sum = total_sum * factor + jnp.sum(exp_terms, axis=-1)
            shaped_values = pair_block[1].reshape(per_micro, span_size, head_count, HEAD)
            summed = summed * jnp.transpose(factor, (0, 2, 1))[..., None] + jnp.einsum(
                "bhqk,bkhe->bqhe",
                exp_terms.astype(jnp.bfloat16),
                shaped_values,
                preferred_element_type=jnp.float32,
            )
            return (new_high, total_sum, summed)

        start_stats = (
            jnp.full((per_micro, head_count, span_size), masked_score, jnp.float32),
            jnp.zeros((per_micro, head_count, span_size), jnp.float32),
        )
        start_sum = jnp.zeros((per_micro, span_size, head_count, HEAD), jnp.float32)

        def online_turn(turn_index, carried):
            pair_block, running = carried
            running = add_online(pair_block, (cycle_index - turn_index) % cycle_size, running)
            return (pass_pairs(pair_block), running)

        pair_block, running = lax.fori_loop(
            0, cycle_size - 1, online_turn, (pair_rows, (start_stats[0], start_stats[1], start_sum))
        )
        highest, total_sum, summed = add_online(pair_block, last_source, running)
        attended = summed / jnp.transpose(total_sum, (0, 2, 1))[..., None]
        log_total = highest + jnp.log(total_sum)
        attended_low = attended.reshape(per_micro, span_size, width).astype(jnp.bfloat16)
        branch_one = jnp.einsum(
            "bcd,de->bce", attended_low, out_weight, preferred_element_type=jnp.float32
        )
        middle = inputs + gate_one * branch_one
        normed_two, norm_back_two = jax.vjp(modulate, middle, norm2_gain, shift_two, scale_two)
        normed_two_low = normed_two.astype(jnp.bfloat16)
        hidden = (
            jnp.einsum("bcd,df->bcf", normed_two_low, up_weight, preferred_element_type=jnp.float32)
            + up_bias
        )
        active, gelu_back = jax.vjp(gelu_tanh, hidden)
        active_low = active.astype(jnp.bfloat16)
        branch_two = (
            jnp.einsum("bcf,fd->bcd", active_low, down_weight, preferred_element_type=jnp.float32)
            + down_bias
        )
        outputs.append((middle + gate_two * branch_two).astype(jnp.bfloat16))
        out_grad = cotangent[picked].astype(jnp.float32)
        gate_two_grad = jnp.sum(out_grad * branch_two, axis=1, keepdims=True)
        branch_two_grad = (gate_two * out_grad).astype(jnp.bfloat16)
        down_grad = jnp.einsum(
            "bcf,bcd->fd", active_low, branch_two_grad, preferred_element_type=jnp.float32
        )
        down_bias_grad = jnp.sum(branch_two_grad.astype(jnp.float32), axis=(0, 1))
        (hidden_grad,) = gelu_back(
            jnp.einsum(
                "bcd,fd->bcf", branch_two_grad, down_weight, preferred_element_type=jnp.float32
            )
        )
        hidden_low = hidden_grad.astype(jnp.bfloat16)
        up_grad = jnp.einsum(
            "bcd,bcf->df", normed_two_low, hidden_low, preferred_element_type=jnp.float32
        )
        up_bias_grad = jnp.sum(hidden_low.astype(jnp.float32), axis=(0, 1))
        middle_part, gain_two_grad, shift_two_grad, scale_two_grad = norm_back_two(
            jnp.einsum("bcf,df->bcd", hidden_low, up_weight, preferred_element_type=jnp.float32)
        )
        middle_grad = out_grad + middle_part
        gate_one_grad = jnp.sum(middle_grad * branch_one, axis=1, keepdims=True)
        branch_one_grad = (gate_one * middle_grad).astype(jnp.bfloat16)
        out_weight_part = jnp.einsum(
            "bcd,bce->de", attended_low, branch_one_grad, preferred_element_type=jnp.float32
        )
        attended_grad = (
            jnp.einsum(
                "bce,de->bcd", branch_one_grad, out_weight, preferred_element_type=jnp.float32
            )
            .astype(jnp.bfloat16)
            .reshape(per_micro, span_size, head_count, HEAD)
        )
        row_delta = jnp.einsum("bqhe,bqhe->bhq", attended_grad.astype(jnp.float32), attended)

        def add_grads(pair_block, source, query_grad):
            scores = key_scores(pair_block[0])
            prob_rows = jnp.where(visible_keys(source), jnp.exp(scores - log_total[..., None]), 0.0)
            shaped_keys = pair_block[0].reshape(per_micro, span_size, head_count, HEAD)
            shaped_values = pair_block[1].reshape(per_micro, span_size, head_count, HEAD)
            value_part = jnp.einsum(
                "bhqk,bqhe->bkhe",
                prob_rows.astype(jnp.bfloat16),
                attended_grad,
                preferred_element_type=jnp.float32,
            )
            prob_grad = jnp.einsum(
                "bqhe,bkhe->bhqk", attended_grad, shaped_values, preferred_element_type=jnp.float32
            )
            score_grad = (prob_rows * (prob_grad - row_delta[..., None])).astype(jnp.bfloat16)
            query_grad = (
                query_grad
                + jnp.einsum(
                    "bhqk,bkhe->bqhe", score_grad, shaped_keys, preferred_element_type=jnp.float32
                )
                * score_scale
            )
            key_part = (
                jnp.einsum(
                    "bhqk,bqhe->bkhe", score_grad, queries, preferred_element_type=jnp.float32
                )
                * score_scale
            )
            return (
                query_grad,
                jnp.stack(
                    [
                        key_part.reshape(per_micro, span_size, width),
                        value_part.reshape(per_micro, span_size, width),
                    ]
                ),
            )

        start_query = jnp.zeros((per_micro, span_size, head_count, HEAD), jnp.float32)

        def grads_turn(turn_index, carried):
            pair_block, grad_block, query_grad = carried
            query_grad, key_value_part = add_grads(
                pair_block, (cycle_index - turn_index) % cycle_size, query_grad
            )
            return (
                pass_pairs_again(pair_block),
                pass_grads(grad_block + key_value_part),
                query_grad,
            )

        start_grads = jnp.zeros((2, per_micro, span_size, width), jnp.float32)
        pair_block, grad_block, query_grad = lax.fori_loop(
            0, cycle_size - 1, grads_turn, (pair_rows, start_grads, start_query)
        )
        query_grad, key_value_part = add_grads(pair_block, last_source, query_grad)
        pair_grads = pass_grads(grad_block + key_value_part)
        query_pre = rotate_back(query_grad, cosine_rows, sine_rows).reshape(
            per_micro, span_size, width
        )
        key_pre = rotate_back(
            pair_grads[0].reshape(per_micro, span_size, head_count, HEAD), cosine_rows, sine_rows
        ).reshape(per_micro, span_size, width)
        joined = jnp.concatenate([query_pre, key_pre, pair_grads[1]], axis=-1).astype(jnp.bfloat16)
        qkv_grad = jnp.einsum("bcd,bce->de", normed_low, joined, preferred_element_type=jnp.float32)
        input_part, gain_one_grad, shift_one_grad, scale_one_grad = norm_back(
            jnp.einsum("bce,de->bcd", joined, qkv_weight, preferred_element_type=jnp.float32)
        )
        input_grads.append((middle_grad + input_part).astype(jnp.bfloat16))
        mod_grad = jnp.concatenate(
            [
                shift_one_grad,
                scale_one_grad,
                gate_one_grad,
                shift_two_grad,
                scale_two_grad,
                gate_two_grad,
            ],
            axis=-1,
        )[:, 0, :]
        ada_grad = jnp.dot(
            mod_grad.T,
            condition[picked],
            precision=lax.Precision.HIGHEST,
            preferred_element_type=jnp.float32,
        )
        ada_bias_grad = jnp.sum(mod_grad, axis=0)
        collected.append(
            (
                ada_grad,
                ada_bias_grad,
                gain_one_grad,
                qkv_grad,
                out_weight_part,
                gain_two_grad,
                up_grad,
                up_bias_grad,
                down_grad,
                down_bias_grad,
            )
        )
    summed = functools.reduce(add_trees, collected)
    finals = lax.psum(
        (
            summed[0],
            summed[1],
            summed[2],
            summed[3],
            summed[4],
            summed[5],
            summed[6],
            summed[7],
            summed[8],
            summed[9],
        ),
        ("wide", "narrow"),
    )
    return (
        jnp.concatenate(outputs, axis=0),
        jnp.concatenate(input_grads, axis=0),
        finals[0],
        finals[1],
        finals[2],
        finals[3],
        finals[4],
        finals[5],
        finals[6],
        finals[7],
        finals[8],
        finals[9],
    )


def solution(mesh):
    in_specs = (
        P("wide", "narrow", None),
        P("wide"),
        P("wide"),
        P("wide", None),
        P(),
        P(),
        P(),
        P(),
        P(),
        P(),
        P(),
        P(),
        P(),
        P(),
        P("wide", "narrow", None),
    )
    out_specs = (
        P("wide", "narrow", None),
        P("wide", "narrow", None),
        P(),
        P(),
        P(),
        P(),
        P(),
        P(),
        P(),
        P(),
        P(),
        P(),
    )
    return jax.shard_map(local, mesh=mesh, in_specs=in_specs, out_specs=out_specs, check_vma=False)
```

profile of v0, /device:TPU:0, one launch (start us, length us, event | category | flops | bytes accessed | tf_op | source)
XLA Modules:
  0.0 1062.0 jit_solution(13036474322672682413)
XLA Ops:
  39.6 66.5 %while.85 = (s32[]{:T(128)}, bf16[2,1,256,768]{2,3,1,0:T(8,128)(2,1)}, f32[1,12,256]{2,1,0:T(8,128)}, f32[1,12,256]{2,1,0:T(8,128)}, f32[1,256,12,64]{1,3,2,0:T(...) while((s32[]{:T(128)}, ...), condition=%wide.region_15.16_spmd.clone, body=%wide.region_12.15_spmd.clone.sunk | while | flops 210586640 | bytes 25119744 | solution.py:195
  48.7 14.7 %collective-permute-done.1 = bf16[2,1,256,768]{2,3,1,0:T(8,128)(2,1)} collective-permute-done((bf16[2,1,256,768]{2,3,1,0:T(8,128)(2,1)S(1)}, bf16[2,1,256,768]{2,3,1,0:T(8,128)(2,1)}, u32[]{:S(2)}, u32[]{:S(2)}) %collective-permute-start.1) | collective-permute-done | bytes 786464 | tf_op jit(solution)/shard_map/while/body/eval_jaxpr/ppermute | solution.py:19
  69.5 15.7 %collective-permute-done.1 = bf16[2,1,256,768]{2,3,1,0:T(8,128)(2,1)} collective-permute-done((bf16[2,1,256,768]{2,3,1,0:T(8,128)(2,1)S(1)}, bf16[2,1,256,768]{2,3,1,0:T(8,128)(2,1)}, u32[]{:S(2)}, u32[]{:S(2)}) %collective-permute-start.1) | collective-permute-done | bytes 786464 | tf_op jit(solution)/shard_map/while/body/eval_jaxpr/ppermute | solution.py:19
  91.3 14.8 %collective-permute-done.1 = bf16[2,1,256,768]{2,3,1,0:T(8,128)(2,1)} collective-permute-done((bf16[2,1,256,768]{2,3,1,0:T(8,128)(2,1)S(1)}, bf16[2,1,256,768]{2,3,1,0:T(8,128)(2,1)}, u32[]{:S(2)}, u32[]{:S(2)}) %collective-permute-start.1) | collective-permute-done | bytes 786464 | tf_op jit(solution)/shard_map/while/body/eval_jaxpr/ppermute | solution.py:19
  108.2 57.2 %while.84 = (s32[]{:T(128)}, bf16[2,1,256,768]{2,3,1,0:T(8,128)(2,1)}, f32[1,12,256]{2,1,0:T(8,128)S(1)}, f32[1,12,256]{2,1,0:T(8,128)}, f32[1,256,12,64]{1,3,2,...) while((s32[]{:T(128)}, ...), condition=%wide.region_5.6_spmd.clone, body=%wide.region_2.5_spmd.clone.sunk | while | flops 210586640 | bytes 25070564 | solution.py:195
  113.6 14.5 %collective-permute-done = bf16[2,1,256,768]{2,3,1,0:T(8,128)(2,1)} collective-permute-done((bf16[2,1,256,768]{2,3,1,0:T(8,128)(2,1)S(1)}, bf16[2,1,256,768]{2,3,1,0:T(8,128)(2,1)}, u32[]{:S(2)}, u32[]{:S(2)}) %collective-permute-start) | collective-permute-done | bytes 786464 | tf_op jit(solution)/shard_map/while/body/eval_jaxpr/ppermute | solution.py:19
  133.5 13.6 %collective-permute-done = bf16[2,1,256,768]{2,3,1,0:T(8,128)(2,1)} collective-permute-done((bf16[2,1,256,768]{2,3,1,0:T(8,128)(2,1)S(1)}, bf16[2,1,256,768]{2,3,1,0:T(8,128)(2,1)}, u32[]{:S(2)}, u32[]{:S(2)}) %collective-permute-start) | collective-permute-done | bytes 786464 | tf_op jit(solution)/shard_map/while/body/eval_jaxpr/ppermute | solution.py:19
  152.5 12.7 %collective-permute-done = bf16[2,1,256,768]{2,3,1,0:T(8,128)(2,1)} collective-permute-done((bf16[2,1,256,768]{2,3,1,0:T(8,128)(2,1)S(1)}, bf16[2,1,256,768]{2,3,1,0:T(8,128)(2,1)}, u32[]{:S(2)}, u32[]{:S(2)}) %collective-permute-start) | collective-permute-done | bytes 786464 | tf_op jit(solution)/shard_map/while/body/eval_jaxpr/ppermute | solution.py:19
  202.8 131.9 %while.86 = (s32[]{:T(128)}, bf16[2,1,256,768]{2,3,1,0:T(8,128)(2,1)}, f32[2,1,256,768]{2,3,1,0:T(8,128)}, f32[1,256,12,64]{1,3,2,0:T(8,128)}, s32[]{:T(128)}, /...) while((s32[]{:T(128)}, ...), condition=%wide.region_23.24_spmd.clone, body=%wide.region_22.23_spmd.clone.sunk | while | flops 513934336 | bytes 45259516 | solution.py:306
  217.1 20.1 %collective-permute-done.3 = bf16[2,1,256,768]{2,3,1,0:T(8,128)(2,1)} collective-permute-done((bf16[2,1,256,768]{2,3,1,0:T(8,128)(2,1)}, bf16[2,1,256,768]{2,3,1,0:T(8,128)(2,1)}, u32[]{:S(2)}, u32[]{:S(2)}) %collective-permute-start.3) | collective-permute-done | bytes 786464 | tf_op jit(solution)/shard_map/while/body/eval_jaxpr/ppermute | solution.py:19
  239.5 8.1 collective-permute-done.2
  262.3 19.8 %collective-permute-done.3 = bf16[2,1,256,768]{2,3,1,0:T(8,128)(2,1)} collective-permute-done((bf16[2,1,256,768]{2,3,1,0:T(8,128)(2,1)}, bf16[2,1,256,768]{2,3,1,0:T(8,128)(2,1)}, u32[]{:S(2)}, u32[]{:S(2)}) %collective-permute-start.3) | collective-permute-done | bytes 786464 | tf_op jit(solution)/shard_map/while/body/eval_jaxpr/ppermute | solution.py:19
  284.5 7.2 collective-permute-done.2
  306.2 19.8 %collective-permute-done.3 = bf16[2,1,256,768]{2,3,1,0:T(8,128)(2,1)} collective-permute-done((bf16[2,1,256,768]{2,3,1,0:T(8,128)(2,1)}, bf16[2,1,256,768]{2,3,1,0:T(8,128)(2,1)}, u32[]{:S(2)}, u32[]{:S(2)}) %collective-permute-start.3) | collective-permute-done | bytes 786464 | tf_op jit(solution)/shard_map/while/body/eval_jaxpr/ppermute | solution.py:19
  348.8 126.2 %while.87 = (s32[]{:T(128)}, bf16[2,1,256,768]{2,3,1,0:T(8,128)(2,1)}, f32[2,1,256,768]{2,3,1,0:T(8,128)}, f32[1,256,12,64]{1,3,2,0:T(8,128)}, s32[]{:T(128)}, /...) while((s32[]{:T(128)}, ...), condition=%wide.region_29.30_spmd.clone, body=%wide.region_28.29_spmd.clone.sunk | while | flops 513934336 | bytes 42212092 | solution.py:306
  360.1 20.4 %collective-permute-done.5 = bf16[2,1,256,768]{2,3,1,0:T(8,128)(2,1)} collective-permute-done((bf16[2,1,256,768]{2,3,1,0:T(8,128)(2,1)}, bf16[2,1,256,768]{2,3,1,0:T(8,128)(2,1)}, u32[]{:S(2)}, u32[]{:S(2)}) %collective-permute-start.5) | collective-permute-done | bytes 786464 | tf_op jit(solution)/shard_map/while/body/eval_jaxpr/ppermute | solution.py:19
  383.0 9.0 collective-permute-done.4
  403.6 19.9 %collective-permute-done.5 = bf16[2,1,256,768]{2,3,1,0:T(8,128)(2,1)} collective-permute-done((bf16[2,1,256,768]{2,3,1,0:T(8,128)(2,1)}, bf16[2,1,256,768]{2,3,1,0:T(8,128)(2,1)}, u32[]{:S(2)}, u32[]{:S(2)}) %collective-permute-start.5) | collective-permute-done | bytes 786464 | tf_op jit(solution)/shard_map/while/body/eval_jaxpr/ppermute | solution.py:19
  425.9 8.0 collective-permute-done.4
  445.5 19.9 %collective-permute-done.5 = bf16[2,1,256,768]{2,3,1,0:T(8,128)(2,1)} collective-permute-done((bf16[2,1,256,768]{2,3,1,0:T(8,128)(2,1)}, bf16[2,1,256,768]{2,3,1,0:T(8,128)(2,1)}, u32[]{:S(2)}, u32[]{:S(2)}) %collective-permute-start.5) | collective-permute-done | bytes 786464 | tf_op jit(solution)/shard_map/while/body/eval_jaxpr/ppermute | solution.py:19
  554.5 7.9 convolution_add_fusion
  573.2 42.2 %all-reduce = (f32[4608]{0:T(1024)}, f32[768]{0:T(1024)}, f32[768]{0:T(1024)}, f32[3072]{0:T(1024)}, f32[768]{0:T(1024)}) all-reduce(f32[4608]{0:T(1024)S(1)} %add.737, f32[768]{0:T(1024)S(1)} %add.738, f32[768]{0:T(1024)} %add.741, f32[3072]{0:T(1024)} %add.743, f32[768]{0:T(1024)} %add.745), channel_id=1, replica_groups=mesh['wide'=8,'narrow'=4] {'wide','narrow'}, use_global_device_ids=true, to_apply=%region_45.46 | all-reduce | flops 9984 | bytes 79872 | tf_op jit(solution)/shard_map/psum | solution.py:356
  620.4 410.0 %all-reduce.4.cloned.1.call-done = (f32[4608,128]{1,0:T(8,128)}, f32[768,2304]{1,0:T(8,128)}, f32[768,768]{1,0:T(8,128)}, f32[768,3072]{1,0:T(8,128)}, f32[3072,768]{1,0:T(8,128)}) async-done(((f32[4608,128]{1,0:T(8,128)}, f32[768,2304]{1,0:T(8,128)}, f32[768,768]{1,0:T(8,128)}, f32[768,3072]{1,0:T(8,128)}, f32[3072,768]{1,0:T(8,128)}), (f32[4608,128]{1,0:T(8,128)}, f32[768,2304]{1,0:T(8,128)}, ...) | async-done | bytes 30670864 | tf_op jit(solution)/shard_map/psum | solution.py:356
  1041.7 9.3 copy.174
  (693 shorter events, 336.6 us)
Async XLA Ops:
  7.2 168.4 %copy-start = (bf16[768,768]{1,0:T(8,128)(2,1)S(1)}, bf16[768,768]{1,0:T(8,128)(2,1)}, u32[]{:S(2)}) copy-start(bf16[768,768]{1,0:T(8,128)(2,1)} %param.31) | copy-start | bytes 3538948
  7.2 1023.2 %all-reduce.4.cloned.1.call-start = ((), (), s32[]{:S(2)}) async-start(), calls=%async_computation | async-start | bytes 61341696 | tf_op jit(solution)/shard_map/psum | solution.py:356
  33.4 74.8 %copy-start.47 = (bf16[1,256,12,32]{1,3,2,0:T(8,128)(2,1)}, bf16[1,256,12,32]{1,3,2,0:T(8,128)(2,1)S(1)}, u32[]{:S(2)}) copy-start(bf16[1,256,12,32]{1,3,2,0:T(8,128)(2,1)S(1)} %get-tuple-element.1423) | copy-start | bytes 589828
  33.4 74.8 %copy-start.49 = (bf16[1,256,12,32]{1,3,2,0:T(8,128)(2,1)}, bf16[1,256,12,32]{1,3,2,0:T(8,128)(2,1)S(1)}, u32[]{:S(2)}) copy-start(bf16[1,256,12,32]{1,3,2,0:T(8,128)(2,1)S(1)} %get-tuple-element.1424) | copy-start | bytes 589828
  40.8 22.7 %collective-permute-start.1 = (bf16[2,1,256,768]{2,3,1,0:T(8,128)(2,1)S(1)}, bf16[2,1,256,768]{2,3,1,0:T(8,128)(2,1)}, u32[]{:S(2)}, u32[]{:S(2)}) collective-permute-start(bf16[2,1,256,768]{2,3,1,0:T(8,128)(2,1)S(1)} %copy.108), channel_id=1, source_target_pairs={{3,0},{0,1},{1,2},{2,3},{7,4},{4,5},{5,6},{6,7},{11,8},{8,9},{9,10... | collective-permute-start | bytes 2359304 | tf_op jit(solution)/shard_map/while/body/eval_jaxpr/ppermute | solution.py:19
  64.6 20.6 %collective-permute-start.1 = (bf16[2,1,256,768]{2,3,1,0:T(8,128)(2,1)S(1)}, bf16[2,1,256,768]{2,3,1,0:T(8,128)(2,1)}, u32[]{:S(2)}, u32[]{:S(2)}) collective-permute-start(bf16[2,1,256,768]{2,3,1,0:T(8,128)(2,1)S(1)} %copy.108), channel_id=1, source_target_pairs={{3,0},{0,1},{1,2},{2,3},{7,4},{4,5},{5,6},{6,7},{11,8},{8,9},{9,10... | collective-permute-start | bytes 2359304 | tf_op jit(solution)/shard_map/while/body/eval_jaxpr/ppermute | solution.py:19
  86.4 19.7 %collective-permute-start.1 = (bf16[2,1,256,768]{2,3,1,0:T(8,128)(2,1)S(1)}, bf16[2,1,256,768]{2,3,1,0:T(8,128)(2,1)}, u32[]{:S(2)}, u32[]{:S(2)}) collective-permute-start(bf16[2,1,256,768]{2,3,1,0:T(8,128)(2,1)S(1)} %copy.108), channel_id=1, source_target_pairs={{3,0},{0,1},{1,2},{2,3},{7,4},{4,5},{5,6},{6,7},{11,8},{8,9},{9,10... | collective-permute-start | bytes 2359304 | tf_op jit(solution)/shard_map/while/body/eval_jaxpr/ppermute | solution.py:19
  109.3 18.8 %collective-permute-start = (bf16[2,1,256,768]{2,3,1,0:T(8,128)(2,1)S(1)}, bf16[2,1,256,768]{2,3,1,0:T(8,128)(2,1)}, u32[]{:S(2)}, u32[]{:S(2)}) collective-permute-start(bf16[2,1,256,768]{2,3,1,0:T(8,128)(2,1)S(1)} %copy.123), channel_id=1, source_target_pairs={{3,0},{0,1},{1,2},{2,3},{7,4},{4,5},{5,6},{6,7},{11,8},{8,9},{9,10... | collective-permute-start | bytes 2359304 | tf_op jit(solution)/shard_map/while/body/eval_jaxpr/ppermute | solution.py:19
  129.2 17.9 %collective-permute-start = (bf16[2,1,256,768]{2,3,1,0:T(8,128)(2,1)S(1)}, bf16[2,1,256,768]{2,3,1,0:T(8,128)(2,1)}, u32[]{:S(2)}, u32[]{:S(2)}) collective-permute-start(bf16[2,1,256,768]{2,3,1,0:T(8,128)(2,1)S(1)} %copy.123), channel_id=1, source_target_pairs={{3,0},{0,1},{1,2},{2,3},{7,4},{4,5},{5,6},{6,7},{11,8},{8,9},{9,10... | collective-permute-start | bytes 2359304 | tf_op jit(solution)/shard_map/while/body/eval_jaxpr/ppermute | solution.py:19
  148.2 16.9 %collective-permute-start = (bf16[2,1,256,768]{2,3,1,0:T(8,128)(2,1)S(1)}, bf16[2,1,256,768]{2,3,1,0:T(8,128)(2,1)}, u32[]{:S(2)}, u32[]{:S(2)}) collective-permute-start(bf16[2,1,256,768]{2,3,1,0:T(8,128)(2,1)S(1)} %copy.123), channel_id=1, source_target_pairs={{3,0},{0,1},{1,2},{2,3},{7,4},{4,5},{5,6},{6,7},{11,8},{8,9},{9,10... | collective-permute-start | bytes 2359304 | tf_op jit(solution)/shard_map/while/body/eval_jaxpr/ppermute | solution.py:19
  214.5 22.6 %collective-permute-start.3 = (bf16[2,1,256,768]{2,3,1,0:T(8,128)(2,1)}, bf16[2,1,256,768]{2,3,1,0:T(8,128)(2,1)}, u32[]{:S(2)}, u32[]{:S(2)}) collective-permute-start(bf16[2,1,256,768]{2,3,1,0:T(8,128)(2,1)} %fusion.436), channel_id=1, source_target_pairs={{3,0},{0,1},{1,2},{2,3},{7,4},{4,5},{5,6},{6,7},{11,8},{8,9},{9,10... | collective-permute-start | bytes 2359304 | tf_op jit(solution)/shard_map/while/body/eval_jaxpr/ppermute | solution.py:19
  214.5 33.1 %collective-permute-start.2 = (bf16[2,1,256,768]{2,3,1,0:T(8,128)(2,1)}, bf16[2,1,256,768]{2,3,1,0:T(8,128)(2,1)}, u32[]{:S(2)}, u32[]{:S(2)}) collective-permute-start(bf16[2,1,256,768]{2,3,1,0:T(8,128)(2,1)} %copy.149), channel_id=1, source_target_pairs={{3,0},{0,1},{1,2},{2,3},{7,4},{4,5},{5,6},{6,7},{11,8},{8,9},{9,10... | collective-permute-start | bytes 2359304 | tf_op jit(solution)/shard_map/while/body/eval_jaxpr/ppermute | solution.py:19
  259.5 22.6 %collective-permute-start.3 = (bf16[2,1,256,768]{2,3,1,0:T(8,128)(2,1)}, bf16[2,1,256,768]{2,3,1,0:T(8,128)(2,1)}, u32[]{:S(2)}, u32[]{:S(2)}) collective-permute-start(bf16[2,1,256,768]{2,3,1,0:T(8,128)(2,1)} %fusion.436), channel_id=1, source_target_pairs={{3,0},{0,1},{1,2},{2,3},{7,4},{4,5},{5,6},{6,7},{11,8},{8,9},{9,10... | collective-permute-start | bytes 2359304 | tf_op jit(solution)/shard_map/while/body/eval_jaxpr/ppermute | solution.py:19
  259.5 32.2 %collective-permute-start.2 = (bf16[2,1,256,768]{2,3,1,0:T(8,128)(2,1)}, bf16[2,1,256,768]{2,3,1,0:T(8,128)(2,1)}, u32[]{:S(2)}, u32[]{:S(2)}) collective-permute-start(bf16[2,1,256,768]{2,3,1,0:T(8,128)(2,1)} %copy.149), channel_id=1, source_target_pairs={{3,0},{0,1},{1,2},{2,3},{7,4},{4,5},{5,6},{6,7},{11,8},{8,9},{9,10... | collective-permute-start | bytes 2359304 | tf_op jit(solution)/shard_map/while/body/eval_jaxpr/ppermute | solution.py:19
  303.4 22.6 %collective-permute-start.3 = (bf16[2,1,256,768]{2,3,1,0:T(8,128)(2,1)}, bf16[2,1,256,768]{2,3,1,0:T(8,128)(2,1)}, u32[]{:S(2)}, u32[]{:S(2)}) collective-permute-start(bf16[2,1,256,768]{2,3,1,0:T(8,128)(2,1)} %fusion.436), channel_id=1, source_target_pairs={{3,0},{0,1},{1,2},{2,3},{7,4},{4,5},{5,6},{6,7},{11,8},{8,9},{9,10... | collective-permute-start | bytes 2359304 | tf_op jit(solution)/shard_map/while/body/eval_jaxpr/ppermute | solution.py:19
  303.4 31.2 %collective-permute-start.2 = (bf16[2,1,256,768]{2,3,1,0:T(8,128)(2,1)}, bf16[2,1,256,768]{2,3,1,0:T(8,128)(2,1)}, u32[]{:S(2)}, u32[]{:S(2)}) collective-permute-start(bf16[2,1,256,768]{2,3,1,0:T(8,128)(2,1)} %copy.149), channel_id=1, source_target_pairs={{3,0},{0,1},{1,2},{2,3},{7,4},{4,5},{5,6},{6,7},{11,8},{8,9},{9,10... | collective-permute-start | bytes 2359304 | tf_op jit(solution)/shard_map/while/body/eval_jaxpr/ppermute | solution.py:19
  344.1 178.0 %collective-permute-start.6 = (bf16[2,1,256,768]{2,3,1,0:T(8,128)(2,1)}, bf16[2,1,256,768]{2,3,1,0:T(8,128)(2,1)}, u32[]{:S(2)}, u32[]{:S(2)}) collective-permute-start(bf16[2,1,256,768]{2,3,1,0:T(8,128)(2,1)} %fusion.114), channel_id=1, source_target_pairs={{3,0},{0,1},{1,2},{2,3},{7,4},{4,5},{5,6},{6,7},{11,8},{8,9},{9,10... | collective-permute-start | bytes 2359304 | tf_op jit(solution)/shard_map/ppermute | solution.py:19
  358.0 22.6 %collective-permute-start.5 = (bf16[2,1,256,768]{2,3,1,0:T(8,128)(2,1)}, bf16[2,1,256,768]{2,3,1,0:T(8,128)(2,1)}, u32[]{:S(2)}, u32[]{:S(2)}) collective-permute-start(bf16[2,1,256,768]{2,3,1,0:T(8,128)(2,1)} %fusion.452), channel_id=1, source_target_pairs={{3,0},{0,1},{1,2},{2,3},{7,4},{4,5},{5,6},{6,7},{11,8},{8,9},{9,10... | collective-permute-start | bytes 2359304 | tf_op jit(solution)/shard_map/while/body/eval_jaxpr/ppermute | solution.py:19
  358.0 33.9 %collective-permute-start.4 = (bf16[2,1,256,768]{2,3,1,0:T(8,128)(2,1)S(1)}, bf16[2,1,256,768]{2,3,1,0:T(8,128)(2,1)}, u32[]{:S(2)}, u32[]{:S(2)}) collective-permute-start(bf16[2,1,256,768]{2,3,1,0:T(8,128)(2,1)S(1)} %copy.137), channel_id=1, source_target_pairs={{3,0},{0,1},{1,2},{2,3},{7,4},{4,5},{5,6},{6,7},{11,8},{8,9},{9,10... | collective-permute-start | bytes 2359304 | tf_op jit(solution)/shard_map/while/body/eval_jaxpr/ppermute | solution.py:19
  400.9 22.6 %collective-permute-start.5 = (bf16[2,1,256,768]{2,3,1,0:T(8,128)(2,1)}, bf16[2,1,256,768]{2,3,1,0:T(8,128)(2,1)}, u32[]{:S(2)}, u32[]{:S(2)}) collective-permute-start(bf16[2,1,256,768]{2,3,1,0:T(8,128)(2,1)} %fusion.452), channel_id=1, source_target_pairs={{3,0},{0,1},{1,2},{2,3},{7,4},{4,5},{5,6},{6,7},{11,8},{8,9},{9,10... | collective-permute-start | bytes 2359304 | tf_op jit(solution)/shard_map/while/body/eval_jaxpr/ppermute | solution.py:19
  400.9 33.0 %collective-permute-start.4 = (bf16[2,1,256,768]{2,3,1,0:T(8,128)(2,1)S(1)}, bf16[2,1,256,768]{2,3,1,0:T(8,128)(2,1)}, u32[]{:S(2)}, u32[]{:S(2)}) collective-permute-start(bf16[2,1,256,768]{2,3,1,0:T(8,128)(2,1)S(1)} %copy.137), channel_id=1, source_target_pairs={{3,0},{0,1},{1,2},{2,3},{7,4},{4,5},{5,6},{6,7},{11,8},{8,9},{9,10... | collective-permute-start | bytes 2359304 | tf_op jit(solution)/shard_map/while/body/eval_jaxpr/ppermute | solution.py:19
  442.8 22.6 %collective-permute-start.5 = (bf16[2,1,256,768]{2,3,1,0:T(8,128)(2,1)}, bf16[2,1,256,768]{2,3,1,0:T(8,128)(2,1)}, u32[]{:S(2)}, u32[]{:S(2)}) collective-permute-start(bf16[2,1,256,768]{2,3,1,0:T(8,128)(2,1)} %fusion.452), channel_id=1, source_target_pairs={{3,0},{0,1},{1,2},{2,3},{7,4},{4,5},{5,6},{6,7},{11,8},{8,9},{9,10... | collective-permute-start | bytes 2359304 | tf_op jit(solution)/shard_map/while/body/eval_jaxpr/ppermute | solution.py:19
  442.8 32.1 %collective-permute-start.4 = (bf16[2,1,256,768]{2,3,1,0:T(8,128)(2,1)S(1)}, bf16[2,1,256,768]{2,3,1,0:T(8,128)(2,1)}, u32[]{:S(2)}, u32[]{:S(2)}) collective-permute-start(bf16[2,1,256,768]{2,3,1,0:T(8,128)(2,1)S(1)} %copy.137), channel_id=1, source_target_pairs={{3,0},{0,1},{1,2},{2,3},{7,4},{4,5},{5,6},{6,7},{11,8},{8,9},{9,10... | collective-permute-start | bytes 2359304 | tf_op jit(solution)/shard_map/while/body/eval_jaxpr/ppermute | solution.py:19
  483.6 39.8 %collective-permute-start.7 = (bf16[2,1,256,768]{2,3,1,0:T(8,128)(2,1)}, bf16[2,1,256,768]{2,3,1,0:T(8,128)(2,1)}, u32[]{:S(2)}, u32[]{:S(2)}) collective-permute-start(bf16[2,1,256,768]{2,3,1,0:T(8,128)(2,1)} %fusion.115), channel_id=1, source_target_pairs={{3,0},{0,1},{1,2},{2,3},{7,4},{4,5},{5,6},{6,7},{11,8},{8,9},{9,10... | collective-permute-start | bytes 2359304 | tf_op jit(solution)/shard_map/ppermute | solution.py:19
  (190 other events, 1021.9 us)
Sparse Core Ops, SparseCore 0:
  565.9 464.4 all-reduce.3
where the time goes:
time: 1070 us; the launch traced here: 1060 us
  waiting for transfers between devices  662 us (62%)
  matrix products  149 us (14%)
  local copies, waits for them, and re-layouts  95.2 us (9%)
  other arithmetic  92.4 us (9%)
  blocking collectives  42.2 us (4%)
  between operations  16.4 us (2%)
    psum x1, waiting for transfers between devices, local(): lax.psum((summed[0], summed[1], summed[2], summed[3], summed[4], summed[5...  410 us
    ppermute x20, waiting for transfers between devices, shifted(): return lax.ppermute(block, axis, route)  251 us
    unnamed x314, local copies, waits for them, and re-layouts  53.2 us
    psum x1, blocking collectives, local(): lax.psum((summed[0], summed[1], summed[2], summed[3], summed[4], summed[5...  42.2 us
  transfers between devices with their start and end apart: 21, of which 19 were waited for; matrix products, arithmetic and copies ran while one was open for 14% of the time, Pallas kernels for 0%

commit v1 on v0

--- a/solution.py
+++ b/solution.py
@@ -11,6 +11,11 @@
 norm_epsilon = 1e-05
 gelu_coeff = 0.7978845608028654
 masked_score = -1e30
+
+
+def one_after_other(x, one, other):
+    partial = lax.psum(x, one)
+    return lax.psum(partial, other)
 
 
 def shifted(block, axis, distance):
@@ -353,7 +358,7 @@
             )
         )
     summed = functools.reduce(add_trees, collected)
-    finals = lax.psum(
+    finals = one_after_other(
         (
             summed[0],
             summed[1],
@@ -366,7 +371,8 @@
             summed[8],
             summed[9],
         ),
-        ("wide", "narrow"),
+        "narrow",
+        "wide",
     )
     return (
         jnp.concatenate(outputs, axis=0),

time: 1070 us -> 2000 us (1.87)
  waiting for transfers between devices: 662 us -> 1590 us
    psum x1 -> x2, waiting for transfers between devices: 410 us -> 1330 us  [the longest x1 1020 us: one_after_other(): partial = lax.psum(x, one)]
    unnamed x314 -> x316, local copies, waits for them, and re-layouts: 53.2 us -> 51.8 us
    psum x1 -> x2, blocking collectives: 42.2 us -> 43.4 us  [the longest x1 25.6 us: one_after_other(): return lax.psum(partial, other)]
  transfers between devices with their start and end apart: 21 -> 22, of which waited for: 19 -> 20; matrix products, arithmetic and copies ran while one was open for 14% -> 7% of each run, Pallas kernels for 0% -> 0%
where the time goes in v1:
time: 2000 us; the launch traced here: 1990 us
  waiting for transfers between devices  1590 us (80%)
  matrix products  149 us (7%)
  local copies, waits for them, and re-layouts  93.1 us (5%)
  other arithmetic  92.4 us (5%)
  blocking collectives  43.4 us (2%)
    psum x1, waiting for transfers between devices, one_after_other(): partial = lax.psum(x, one)  1020 us
    psum x1, waiting for transfers between devices, one_after_other(): return lax.psum(partial, other)  319 us
    ppermute x20, waiting for transfers between devices, shifted(): return lax.ppermute(block, axis, route)  251 us
    unnamed x316, local copies, waits for them, and re-layouts  51.8 us
  transfers between devices with their start and end apart: 22, of which 20 were waited for; matrix products, arithmetic and copies ran while one was open for 7% of the time, Pallas kernels for 0%

profile of v1, /device:TPU:0, one launch (start us, length us, event | category | flops | bytes accessed | tf_op | source)
XLA Modules:
  0.0 1985.0 jit_solution(13095081780040925473)
XLA Ops:
  38.2 66.4 %while.85 = (s32[]{:T(128)}, bf16[2,1,256,768]{2,3,1,0:T(8,128)(2,1)}, f32[1,12,256]{2,1,0:T(8,128)}, f32[1,12,256]{2,1,0:T(8,128)}, f32[1,256,12,64]{1,3,2,0:T(...) while((s32[]{:T(128)}, ...), condition=%wide.region_15.16_spmd.clone, body=%wide.region_12.15_spmd.clone.sunk | while | flops 210586640 | bytes 25119744 | solution.py:200
  47.2 14.8 collective-permute-done.1
  68.0 15.7 collective-permute-done.1
  89.8 14.8 collective-permute-done.1
  106.7 57.2 %while.84 = (s32[]{:T(128)}, bf16[2,1,256,768]{2,3,1,0:T(8,128)(2,1)}, f32[1,12,256]{2,1,0:T(8,128)S(1)}, f32[1,12,256]{2,1,0:T(8,128)}, f32[1,256,12,64]{1,3,2,...) while((s32[]{:T(128)}, ...), condition=%wide.region_5.6_spmd.clone, body=%wide.region_2.5_spmd.clone.sunk | while | flops 210586640 | bytes 25070564 | solution.py:200
  112.1 14.5 collective-permute-done
  132.1 13.6 collective-permute-done
  151.0 12.7 collective-permute-done
  201.3 131.9 %while.86 = (s32[]{:T(128)}, bf16[2,1,256,768]{2,3,1,0:T(8,128)(2,1)}, f32[2,1,256,768]{2,3,1,0:T(8,128)}, f32[1,256,12,64]{1,3,2,0:T(8,128)}, s32[]{:T(128)}, /...) while((s32[]{:T(128)}, ...), condition=%wide.region_23.24_spmd.clone, body=%wide.region_22.23_spmd.clone.sunk | while | flops 513934336 | bytes 45259516 | solution.py:311
  215.6 20.1 %collective-permute-done.3 = bf16[2,1,256,768]{2,3,1,0:T(8,128)(2,1)} collective-permute-done((bf16[2,1,256,768]{2,3,1,0:T(8,128)(2,1)}, bf16[2,1,256,768]{2,3,1,0:T(8,128)(2,1)}, u32[]{:S(2)}, u32[]{:S(2)}) %collective-permute-start.3) | collective-permute-done | bytes 786464 | tf_op jit(solution)/shard_map/while/body/eval_jaxpr/ppermute | solution.py:24
  238.0 8.1 collective-permute-done.2
  260.7 19.8 collective-permute-done.3
  304.7 19.8 collective-permute-done.3
  346.9 125.6 %while.87 = (s32[]{:T(128)}, bf16[2,1,256,768]{2,3,1,0:T(8,128)(2,1)}, f32[2,1,256,768]{2,3,1,0:T(8,128)}, f32[1,256,12,64]{1,3,2,0:T(8,128)}, s32[]{:T(128)}, /...) while((s32[]{:T(128)}, ...), condition=%wide.region_29.30_spmd.clone, body=%wide.region_28.29_spmd.clone.sunk | while | flops 513934336 | bytes 42212092 | solution.py:311
  358.0 20.6 %collective-permute-done.5 = bf16[2,1,256,768]{2,3,1,0:T(8,128)(2,1)} collective-permute-done((bf16[2,1,256,768]{2,3,1,0:T(8,128)(2,1)}, bf16[2,1,256,768]{2,3,1,0:T(8,128)(2,1)}, u32[]{:S(2)}, u32[]{:S(2)}) %collective-permute-start.5) | collective-permute-done | bytes 786464 | tf_op jit(solution)/shard_map/while/body/eval_jaxpr/ppermute | solution.py:24
  381.0 8.8 collective-permute-done.4
  401.4 19.9 %collective-permute-done.5 = bf16[2,1,256,768]{2,3,1,0:T(8,128)(2,1)} collective-permute-done((bf16[2,1,256,768]{2,3,1,0:T(8,128)(2,1)}, bf16[2,1,256,768]{2,3,1,0:T(8,128)(2,1)}, u32[]{:S(2)}, u32[]{:S(2)}) %collective-permute-start.5) | collective-permute-done | bytes 786464 | tf_op jit(solution)/shard_map/while/body/eval_jaxpr/ppermute | solution.py:24
  443.3 19.9 %collective-permute-done.5 = bf16[2,1,256,768]{2,3,1,0:T(8,128)(2,1)} collective-permute-done((bf16[2,1,256,768]{2,3,1,0:T(8,128)(2,1)}, bf16[2,1,256,768]{2,3,1,0:T(8,128)(2,1)}, u32[]{:S(2)}, u32[]{:S(2)}) %collective-permute-start.5) | collective-permute-done | bytes 786464 | tf_op jit(solution)/shard_map/while/body/eval_jaxpr/ppermute | solution.py:24
  552.0 7.9 convolution_add_fusion
  563.4 1015.1 %all-reduce.9.cloned.1.call-done = (f32[4608,128]{1,0:T(8,128)}, f32[768,2304]{1,0:T(8,128)}, f32[768,768]{1,0:T(8,128)}, f32[768,3072]{1,0:T(8,128)}, f32[3072,768]{1,0:T(8,128)}) async-done(((f32[4608,128]{1,0:T(8,128)}, f32[768,2304]{1,0:T(8,128)}, f32[768,768]{1,0:T(8,128)}, f32[768,3072]{1,0:T(8,128)}, f32[3072,768]{1,0:T(8,128)}), (f32[4608,128]{1,0:T(8,128)}, f32[768,2304]{1,0:T(8,128)}, ...) | async-done | bytes 30670864 | tf_op jit(solution)/shard_map/psum | solution.py:17
  1585.9 17.8 all-reduce.2
  1603.7 25.6 %all-reduce = (f32[4608]{0:T(1024)}, f32[768]{0:T(1024)}, f32[768]{0:T(1024)}, f32[3072]{0:T(1024)}, f32[768]{0:T(1024)}) all-reduce(f32[4608]{0:T(1024)S(1)} %get-tuple-element.1387, f32[768]{0:T(1024)S(1)} %get-tuple-element.1388, f32[768]{0:T(1024)S(1)} %get-tuple-element.1389, ...), channel_id=1, replica_groups=mesh['wide'=8,'narrow'=4] {'wide'}, use_global_device_ids=true, to_apply=%region_47.48 | all-reduce | flops 9984 | bytes 79872 | tf_op jit(solution)/shard_map/psum | solution.py:18
  1634.3 319.2 %all-reduce.7.cloned.1.call-done = (f32[4608,128]{1,0:T(8,128)}, f32[768,2304]{1,0:T(8,128)}, f32[768,768]{1,0:T(8,128)}, f32[768,3072]{1,0:T(8,128)}, f32[3072,768]{1,0:T(8,128)}) async-done(((f32[4608,128]{1,0:T(8,128)}, f32[768,2304]{1,0:T(8,128)}, f32[768,768]{1,0:T(8,128)}, f32[768,3072]{1,0:T(8,128)}, f32[3072,768]{1,0:T(8,128)}), (f32[4608,128]{1,0:T(8,128)}, f32[768,2304]{1,0:T(8,128)}, ...) | async-done | bytes 30670864 | tf_op jit(solution)/shard_map/psum | solution.py:18
  1964.7 9.3 copy.179
  (699 shorter events, 349.2 us)
Async XLA Ops:
  7.2 166.9 %copy-start = (bf16[768,768]{1,0:T(8,128)(2,1)S(1)}, bf16[768,768]{1,0:T(8,128)(2,1)}, u32[]{:S(2)}) copy-start(bf16[768,768]{1,0:T(8,128)(2,1)} %param.31) | copy-start | bytes 3538948
  7.2 1571.3 %all-reduce.9.cloned.1.call-start = ((), (), s32[]{:S(2)}) async-start(), calls=%async_computation.1 | async-start | bytes 61341696 | tf_op jit(solution)/shard_map/psum | solution.py:17
  31.9 74.8 %copy-start.47 = (bf16[1,256,12,32]{1,3,2,0:T(8,128)(2,1)}, bf16[1,256,12,32]{1,3,2,0:T(8,128)(2,1)S(1)}, u32[]{:S(2)}) copy-start(bf16[1,256,12,32]{1,3,2,0:T(8,128)(2,1)S(1)} %get-tuple-element.1433) | copy-start | bytes 589828
  39.3 22.7 %collective-permute-start.1 = (bf16[2,1,256,768]{2,3,1,0:T(8,128)(2,1)S(1)}, bf16[2,1,256,768]{2,3,1,0:T(8,128)(2,1)}, u32[]{:S(2)}, u32[]{:S(2)}) collective-permute-start(bf16[2,1,256,768]{2,3,1,0:T(8,128)(2,1)S(1)} %copy.108), channel_id=1, source_target_pairs={{3,0},{0,1},{1,2},{2,3},{7,4},{4,5},{5,6},{6,7},{11,8},{8,9},{9,10... | collective-permute-start | bytes 2359304 | tf_op jit(solution)/shard_map/while/body/eval_jaxpr/ppermute | solution.py:24
  63.2 20.6 %collective-permute-start.1 = (bf16[2,1,256,768]{2,3,1,0:T(8,128)(2,1)S(1)}, bf16[2,1,256,768]{2,3,1,0:T(8,128)(2,1)}, u32[]{:S(2)}, u32[]{:S(2)}) collective-permute-start(bf16[2,1,256,768]{2,3,1,0:T(8,128)(2,1)S(1)} %copy.108), channel_id=1, source_target_pairs={{3,0},{0,1},{1,2},{2,3},{7,4},{4,5},{5,6},{6,7},{11,8},{8,9},{9,10... | collective-permute-start | bytes 2359304 | tf_op jit(solution)/shard_map/while/body/eval_jaxpr/ppermute | solution.py:24
  84.9 19.7 collective-permute-start.1
  107.9 18.8 collective-permute-start
  127.8 17.9 collective-permute-start
  146.8 16.9 collective-permute-start
  213.0 22.6 %collective-permute-start.3 = (bf16[2,1,256,768]{2,3,1,0:T(8,128)(2,1)}, bf16[2,1,256,768]{2,3,1,0:T(8,128)(2,1)}, u32[]{:S(2)}, u32[]{:S(2)}) collective-permute-start(bf16[2,1,256,768]{2,3,1,0:T(8,128)(2,1)} %fusion.436), channel_id=1, source_target_pairs={{3,0},{0,1},{1,2},{2,3},{7,4},{4,5},{5,6},{6,7},{11,8},{8,9},{9,10... | collective-permute-start | bytes 2359304 | tf_op jit(solution)/shard_map/while/body/eval_jaxpr/ppermute | solution.py:24
  213.0 33.1 %collective-permute-start.2 = (bf16[2,1,256,768]{2,3,1,0:T(8,128)(2,1)}, bf16[2,1,256,768]{2,3,1,0:T(8,128)(2,1)}, u32[]{:S(2)}, u32[]{:S(2)}) collective-permute-start(bf16[2,1,256,768]{2,3,1,0:T(8,128)(2,1)} %copy.149), channel_id=1, source_target_pairs={{3,0},{0,1},{1,2},{2,3},{7,4},{4,5},{5,6},{6,7},{11,8},{8,9},{9,10... | collective-permute-start | bytes 2359304 | tf_op jit(solution)/shard_map/while/body/eval_jaxpr/ppermute | solution.py:24
  257.9 22.6 %collective-permute-start.3 = (bf16[2,1,256,768]{2,3,1,0:T(8,128)(2,1)}, bf16[2,1,256,768]{2,3,1,0:T(8,128)(2,1)}, u32[]{:S(2)}, u32[]{:S(2)}) collective-permute-start(bf16[2,1,256,768]{2,3,1,0:T(8,128)(2,1)} %fusion.436), channel_id=1, source_target_pairs={{3,0},{0,1},{1,2},{2,3},{7,4},{4,5},{5,6},{6,7},{11,8},{8,9},{9,10... | collective-permute-start | bytes 2359304 | tf_op jit(solution)/shard_map/while/body/eval_jaxpr/ppermute | solution.py:24
  257.9 32.2 %collective-permute-start.2 = (bf16[2,1,256,768]{2,3,1,0:T(8,128)(2,1)}, bf16[2,1,256,768]{2,3,1,0:T(8,128)(2,1)}, u32[]{:S(2)}, u32[]{:S(2)}) collective-permute-start(bf16[2,1,256,768]{2,3,1,0:T(8,128)(2,1)} %copy.149), channel_id=1, source_target_pairs={{3,0},{0,1},{1,2},{2,3},{7,4},{4,5},{5,6},{6,7},{11,8},{8,9},{9,10... | collective-permute-start | bytes 2359304 | tf_op jit(solution)/shard_map/while/body/eval_jaxpr/ppermute | solution.py:24
  301.9 22.6 %collective-permute-start.3 = (bf16[2,1,256,768]{2,3,1,0:T(8,128)(2,1)}, bf16[2,1,256,768]{2,3,1,0:T(8,128)(2,1)}, u32[]{:S(2)}, u32[]{:S(2)}) collective-permute-start(bf16[2,1,256,768]{2,3,1,0:T(8,128)(2,1)} %fusion.436), channel_id=1, source_target_pairs={{3,0},{0,1},{1,2},{2,3},{7,4},{4,5},{5,6},{6,7},{11,8},{8,9},{9,10... | collective-permute-start | bytes 2359304 | tf_op jit(solution)/shard_map/while/body/eval_jaxpr/ppermute | solution.py:24
  301.9 31.2 %collective-permute-start.2 = (bf16[2,1,256,768]{2,3,1,0:T(8,128)(2,1)}, bf16[2,1,256,768]{2,3,1,0:T(8,128)(2,1)}, u32[]{:S(2)}, u32[]{:S(2)}) collective-permute-start(bf16[2,1,256,768]{2,3,1,0:T(8,128)(2,1)} %copy.149), channel_id=1, source_target_pairs={{3,0},{0,1},{1,2},{2,3},{7,4},{4,5},{5,6},{6,7},{11,8},{8,9},{9,10... | collective-permute-start | bytes 2359304 | tf_op jit(solution)/shard_map/while/body/eval_jaxpr/ppermute | solution.py:24
  342.0 177.7 %collective-permute-start.6 = (bf16[2,1,256,768]{2,3,1,0:T(8,128)(2,1)}, bf16[2,1,256,768]{2,3,1,0:T(8,128)(2,1)}, u32[]{:S(2)}, u32[]{:S(2)}) collective-permute-start(bf16[2,1,256,768]{2,3,1,0:T(8,128)(2,1)} %fusion.114), channel_id=1, source_target_pairs={{3,0},{0,1},{1,2},{2,3},{7,4},{4,5},{5,6},{6,7},{11,8},{8,9},{9,10... | collective-permute-start | bytes 2359304 | tf_op jit(solution)/shard_map/ppermute | solution.py:24
  356.0 22.6 %collective-permute-start.5 = (bf16[2,1,256,768]{2,3,1,0:T(8,128)(2,1)}, bf16[2,1,256,768]{2,3,1,0:T(8,128)(2,1)}, u32[]{:S(2)}, u32[]{:S(2)}) collective-permute-start(bf16[2,1,256,768]{2,3,1,0:T(8,128)(2,1)} %fusion.452), channel_id=1, source_target_pairs={{3,0},{0,1},{1,2},{2,3},{7,4},{4,5},{5,6},{6,7},{11,8},{8,9},{9,10... | collective-permute-start | bytes 2359304 | tf_op jit(solution)/shard_map/while/body/eval_jaxpr/ppermute | solution.py:24
  356.0 33.8 %collective-permute-start.4 = (bf16[2,1,256,768]{2,3,1,0:T(8,128)(2,1)S(1)}, bf16[2,1,256,768]{2,3,1,0:T(8,128)(2,1)}, u32[]{:S(2)}, u32[]{:S(2)}) collective-permute-start(bf16[2,1,256,768]{2,3,1,0:T(8,128)(2,1)S(1)} %copy.137), channel_id=1, source_target_pairs={{3,0},{0,1},{1,2},{2,3},{7,4},{4,5},{5,6},{6,7},{11,8},{8,9},{9,10... | collective-permute-start | bytes 2359304 | tf_op jit(solution)/shard_map/while/body/eval_jaxpr/ppermute | solution.py:24
  398.7 22.6 %collective-permute-start.5 = (bf16[2,1,256,768]{2,3,1,0:T(8,128)(2,1)}, bf16[2,1,256,768]{2,3,1,0:T(8,128)(2,1)}, u32[]{:S(2)}, u32[]{:S(2)}) collective-permute-start(bf16[2,1,256,768]{2,3,1,0:T(8,128)(2,1)} %fusion.452), channel_id=1, source_target_pairs={{3,0},{0,1},{1,2},{2,3},{7,4},{4,5},{5,6},{6,7},{11,8},{8,9},{9,10... | collective-permute-start | bytes 2359304 | tf_op jit(solution)/shard_map/while/body/eval_jaxpr/ppermute | solution.py:24
  398.8 32.9 %collective-permute-start.4 = (bf16[2,1,256,768]{2,3,1,0:T(8,128)(2,1)S(1)}, bf16[2,1,256,768]{2,3,1,0:T(8,128)(2,1)}, u32[]{:S(2)}, u32[]{:S(2)}) collective-permute-start(bf16[2,1,256,768]{2,3,1,0:T(8,128)(2,1)S(1)} %copy.137), channel_id=1, source_target_pairs={{3,0},{0,1},{1,2},{2,3},{7,4},{4,5},{5,6},{6,7},{11,8},{8,9},{9,10... | collective-permute-start | bytes 2359304 | tf_op jit(solution)/shard_map/while/body/eval_jaxpr/ppermute | solution.py:24
  440.6 22.6 %collective-permute-start.5 = (bf16[2,1,256,768]{2,3,1,0:T(8,128)(2,1)}, bf16[2,1,256,768]{2,3,1,0:T(8,128)(2,1)}, u32[]{:S(2)}, u32[]{:S(2)}) collective-permute-start(bf16[2,1,256,768]{2,3,1,0:T(8,128)(2,1)} %fusion.452), channel_id=1, source_target_pairs={{3,0},{0,1},{1,2},{2,3},{7,4},{4,5},{5,6},{6,7},{11,8},{8,9},{9,10... | collective-permute-start | bytes 2359304 | tf_op jit(solution)/shard_map/while/body/eval_jaxpr/ppermute | solution.py:24
  440.6 31.9 %collective-permute-start.4 = (bf16[2,1,256,768]{2,3,1,0:T(8,128)(2,1)S(1)}, bf16[2,1,256,768]{2,3,1,0:T(8,128)(2,1)}, u32[]{:S(2)}, u32[]{:S(2)}) collective-permute-start(bf16[2,1,256,768]{2,3,1,0:T(8,128)(2,1)S(1)} %copy.137), channel_id=1, source_target_pairs={{3,0},{0,1},{1,2},{2,3},{7,4},{4,5},{5,6},{6,7},{11,8},{8,9},{9,10... | collective-permute-start | bytes 2359304 | tf_op jit(solution)/shard_map/while/body/eval_jaxpr/ppermute | solution.py:24
  481.4 39.7 %collective-permute-start.7 = (bf16[2,1,256,768]{2,3,1,0:T(8,128)(2,1)}, bf16[2,1,256,768]{2,3,1,0:T(8,128)(2,1)}, u32[]{:S(2)}, u32[]{:S(2)}) collective-permute-start(bf16[2,1,256,768]{2,3,1,0:T(8,128)(2,1)} %fusion.115), channel_id=1, source_target_pairs={{3,0},{0,1},{1,2},{2,3},{7,4},{4,5},{5,6},{6,7},{11,8},{8,9},{9,10... | collective-permute-start | bytes 2359304 | tf_op jit(solution)/shard_map/ppermute | solution.py:24
  563.3 1390.2 %all-reduce.7.cloned.1.call-start = ((), (), s32[]{:S(2)}) async-start(), calls=%async_computation | async-start | bytes 61341696 | tf_op jit(solution)/shard_map/psum | solution.py:18
  (192 other events, 1118.6 us)
Sparse Core Ops, SparseCore 0:
  563.4 1014.9 all-reduce.8
  1583.9 369.5 all-reduce.6
